TPU v7x, 32 devices: a whole 2x2x4 slice. The times are simulated.
32 devices in a mesh: tx: 2 (over x), ty: 4 (over z), pg: 4 (over y, core).
Axes of the slice: x: 2, y: 2, z: 4, core: 2. Of those that a mesh axis runs over, the one named last changes fastest.
Arguments:
- direct_modes: bfloat16 [64, 3, 32, 512], P('pg', None, 'tx', 'ty'), may hold values from -6 to 6
- adjoint_modes: bfloat16 [64, 3, 32, 512], P(None, None, 'tx', 'ty'), may hold values from -6 to 6
- block_order: int32 [8], replicated, may hold values from 0 to 7, each once
Outputs:
- tensor: float32 [64, 64, 64], P('pg', 'ty', 'tx')
Inputs may be any that keep to these rules, and one draw needn't show every extreme that they name: `block_order`: each of the 8 blocks appears exactly once.
All inputs are finite; a program needn't handle non-finite values.
Results may differ from a plain program's by a relative error of at most 0.0043.
Values may be sent and summed in bfloat16 or wider, within the bound.
A program may use at most 64 MiB of HBM per device.

v0:
```python
import math

import jax
import jax.numpy as jnp
from jax import lax
from jax.sharding import PartitionSpec as P

NBLK = 8
JB = 4
CZ = 4


def extended(block, sides, width):
    for axis, dim in sides:
        count = lax.axis_size(axis)
        forward = [(i, i + 1) for i in range(count - 1)]
        backward = [(target, source) for source, target in forward]
        low = lax.ppermute(
            lax.slice_in_dim(block, block.shape[dim] - width, None, axis=dim), axis, forward
        )
        high = lax.ppermute(lax.slice_in_dim(block, 0, width, axis=dim), axis, backward)
        block = jnp.concatenate([low, block, high], axis=dim)
    return block


def depth_slope(values, depth):
    position = jnp.arange(values.shape[-1]) % depth
    upper = jnp.where(
        position == depth - 1, jnp.roll(values, depth - 1, -1), jnp.roll(values, -1, -1)
    )
    lower = jnp.where(position == 0, jnp.roll(values, 1 - depth, -1), jnp.roll(values, 1, -1))
    return (upper - lower) * 0.5


def slopes(values, wide_x, wide_y, depth):
    along_x = (wide_x[:, :, 2:] - wide_x[:, :, :-2]) * 0.5
    along_y = (wide_y[..., 2 * depth :] - wide_y[..., : -2 * depth]) * 0.5
    along_z = depth_slope(values, depth)
    return jnp.stack([along_x, along_y, along_z], 1).astype(jnp.bfloat16)


def pair_terms(rows_u, rows_g, cols_u, cols_g):
    result = jnp.zeros((rows_u.shape[0], cols_u.shape[0]) + cols_g.shape[2:], jnp.float32)
    for direction in range(3):
        result = result + rows_u[:, None, direction, None] * cols_g[None, :, direction]
        result = result + cols_u[None, :, direction, None] * rows_g[:, None, direction]
    return result.astype(jnp.bfloat16)


def project(pairs, adjoint):
    flat = pairs.reshape(pairs.shape[0] * pairs.shape[1], -1)
    basis = adjoint.reshape(adjoint.shape[0], -1)
    product = lax.dot_general(
        flat, basis, (((1,), (1,)), ((), ())), preferred_element_type=jnp.float32
    )
    return product.reshape(pairs.shape[0], pairs.shape[1], adjoint.shape[0])


def block_tensor(rows_u, rows_g, modes, grads, adjoint, width):
    count = modes.shape[0] // width

    def one_block(start):
        cols_u = lax.dynamic_slice_in_dim(modes, start, width, 0).astype(jnp.float32)
        cols_g = lax.dynamic_slice_in_dim(grads, start, width, 0).astype(jnp.float32)
        return project(pair_terms(rows_u, rows_g, cols_u, cols_g), adjoint)

    starts = jnp.arange(count) * width
    pieces = lax.map(one_block, starts)
    return jnp.transpose(pieces, (1, 0, 2, 3)).reshape(
        rows_u.shape[0], modes.shape[0], adjoint.shape[0]
    )


def shards(direct_modes, adjoint_modes, block_order):
    x_count = lax.axis_size("tx")
    y_count = lax.axis_size("ty")
    group_count = lax.axis_size("pg")
    weight = 1.0 / math.sqrt(
        3.0 * direct_modes.shape[2] * x_count * direct_modes.shape[3] * y_count
    )
    whole = lax.all_gather(direct_modes, "pg", axis=0, tiled=True)
    wide_x = extended(whole, (("tx", 2),), 1)
    wide_y = extended(whole, (("ty", 3),), CZ)
    grads = slopes(
        whole.astype(jnp.float32), wide_x.astype(jnp.float32), wide_y.astype(jnp.float32), CZ
    )
    mode_count = whole.shape[0]
    block_rows = mode_count // NBLK
    per_group = NBLK // group_count
    group_id = lax.axis_index("pg")
    mine = lax.dynamic_slice_in_dim(block_order, group_id * per_group, per_group, 0)
    row_index = (
        mine[:, None] * block_rows + jnp.arange(block_rows, dtype=jnp.int32)[None, :]
    ).reshape(-1)
    rows_u = jnp.take(whole, row_index, axis=0).astype(jnp.float32)
    rows_g = jnp.take(grads, row_index, axis=0).astype(jnp.float32)
    partial_sum = block_tensor(rows_u, rows_g, whole, grads, adjoint_modes, JB) * weight
    row_count = partial_sum.shape[0]
    j_width = mode_count // y_count
    k_width = adjoint_modes.shape[0] // x_count
    arranged = partial_sum.reshape(row_count, y_count, j_width, x_count, k_width)
    arranged = jnp.transpose(arranged, (0, 3, 1, 2, 4)).reshape(row_count, -1)
    shares = lax.psum_scatter(arranged, ("tx", "ty"), scatter_dimension=1, tiled=True)
    return shares.reshape(row_count, j_width, k_width)


def solution(mesh):
    placed = (P("pg", None, "tx", "ty"), P(None, None, "tx", "ty"), P())
    return jax.shard_map(
        shards, mesh=mesh, in_specs=placed, out_specs=P("pg", "ty", "tx"), check_vma=False
    )
```

profile of v0, /device:TPU:0, one launch (start us, length us, event | category | flops | bytes accessed | tf_op | source)
XLA Modules:
  0.0 225.4 jit_solution(8822786861770706708)
XLA Ops:
  6.5 10.3 %all_gather.3 = bf16[64,3,16,128]{3,2,1,0:T(8,128)(2,1)S(1)} all-gather(bf16[16,3,16,128]{3,2,1,0:T(8,128)(2,1)} %param.5), channel_id=1, replica_groups=mesh['tx'=2,'ty'=4,'pg'=4] {'pg'}, dimensions={0}, use_global_device_ids=true | all-gather | bytes 983040 | tf_op jit(solution)/shard_map/all_gather | solution.py:81
  18.4 4.1 %collective-permute-start.2 = (bf16[64,3,16,4]{0,2,3,1:T(8,128)(2,1)}, bf16[64,3,16,4]{0,2,3,1:T(8,128)(2,1)}, u32[]{:S(2)}, u32[]{:S(2)}) collective-permute-start(bf16[64,3,16,4]{0,2,3,1:T(8,128)(2,1)} %copy.25), channel_id=1, source_target_pairs={{0,4},{4,8},{8,12},{1,5},{5,9},{9,13},{2,6},{6,10},{10,14},{3,7},{... | collective-permute-start | bytes 73736 | tf_op jit(solution)/shard_map/ppermute | solution.py:18
  25.9 4.0 %collective-permute-start = (bf16[64,3,1,128]{3,2,1,0:T(2,128)(2,1)}, bf16[64,3,1,128]{3,2,1,0:T(2,128)(2,1)}, u32[]{:S(2)}, u32[]{:S(2)}) collective-permute-start(bf16[64,3,1,128]{3,2,1,0:T(2,128)(2,1)} %get-tuple-element.106), channel_id=1, source_target_pairs={{0,16},{1,17},{2,18},{3,19},{4,20},{5,21},{6,22},{7,23},{8,24},{9,... | collective-permute-start | bytes 147464 | tf_op jit(solution)/shard_map/ppermute | solution.py:18
  30.0 1.5 collective-permute-start.1
  31.6 2.2 slice_bitcast_fusion.12
  33.7 2.1 slice_bitcast_fusion.14
  35.9 2.2 slice_bitcast_fusion.13
  38.1 1.5 fusion.28
  39.9 2.0 copy.29
  41.9 1.8 copy.30
  44.4 1.8 copy.32
  46.9 6.8 %fusion.21 = bf16[64,1,3,16,128]{4,3,2,1,0:T(8,128)(2,1)} fusion(f32[64,1,3,16,125]{4,3,2,0,1:T(8,128)} %get-tuple-element.103, f32[64,1,3,16,3]{4,3,2,0,1:T(8,128)} %get-tuple-element.105, f32[64,1,3,16,1]{4,3,2,0,1:T(8,128)S(1)} %copy-done, f32[64,1,3,16,127]{4,3,2,0,1:T(8,128)} %get-tuple-element.101, f32[64,1,3,16,3]{4,3,2,0,1:T(8,128)} %get-tuple-element.104, ...), kind=kLoop, calls=%fused_computation.52 | loop fusion | flops 3538944 | bytes 7078144 | tf_op jit(solution)/shard_map/convert.2
  54.9 1.5 copy.27
  56.4 1.5 copy.28
  59.3 1.6 maximum_convert_fusion.1
  62.3 1.6 gather_fusion.1
  66.2 82.4 %while.10 = (s32[]{:T(128)}, f32[16,16,4,64]{3,1,2,0:T(8,128)}, f32[16,3,16,128]{3,0,2,1:T(8,128)S(1)}, s32[16]{0:T(128)S(1)}, bf16[64,3,3,16,128]{4,3,2,1,0:T(8...) while((s32[]{:T(128)}, f32[16,16,4,64]{3,1,2,0:T(8,128)}, ...), condition=%wide.region_1.2_spmd, body=%wide.region_0.1_spmd.sunk | while | flops 55148548 | bytes 7307939 | solution.py:68
  85.4 1.5 fusion.32
  100.8 1.5 fusion.32
  116.3 1.5 fusion.32
  131.7 1.5 fusion.32
  147.1 1.5 fusion.32
  152.2 64.9 %reduce-scatter.2.cloned.1.call-done = f32[16,512]{1,0:T(8,128)} async-done(((f32[16,4096]{1,0:T(8,128)}), f32[16,512]{1,0:T(8,128)}) %reduce-scatter.2.cloned.1.call-update) | async-done | bytes 32784 | tf_op jit(solution)/shard_map/reduce_scatter | solution.py:103
  217.1 1.5 reshape.223
  (172 shorter events, 59.9 us)
Async XLA Ops:
  6.5 210.5 %reduce-scatter.2.cloned.1.call-start = ((), (), s32[]{:S(2)}) async-start(), calls=%async_computation.1 | async-start | bytes 294912 | tf_op jit(solution)/shard_map/reduce_scatter | solution.py:103
  18.4 36.5 %collective-permute-start.2 = (bf16[64,3,16,4]{0,2,3,1:T(8,128)(2,1)}, bf16[64,3,16,4]{0,2,3,1:T(8,128)(2,1)}, u32[]{:S(2)}, u32[]{:S(2)}) collective-permute-start(bf16[64,3,16,4]{0,2,3,1:T(8,128)(2,1)} %copy.25), channel_id=1, source_target_pairs={{0,4},{4,8},{8,12},{1,5},{5,9},{9,13},{2,6},{6,10},{10,14},{3,7},{... | collective-permute-start | bytes 73736 | tf_op jit(solution)/shard_map/ppermute | solution.py:18
  23.8 32.6 %collective-permute-start.3 = (bf16[64,3,16,4]{0,2,3,1:T(8,128)(2,1)}, bf16[64,3,16,4]{0,2,3,1:T(8,128)(2,1)}, u32[]{:S(2)}, u32[]{:S(2)}) collective-permute-start(bf16[64,3,16,4]{0,2,3,1:T(8,128)(2,1)} %copy.26), channel_id=1, source_target_pairs={{4,0},{8,4},{12,8},{5,1},{9,5},{13,9},{6,2},{10,6},{14,10},{7,3},{... | collective-permute-start | bytes 73736 | tf_op jit(solution)/shard_map/ppermute | solution.py:21
  25.9 33.3 %collective-permute-start = (bf16[64,3,1,128]{3,2,1,0:T(2,128)(2,1)}, bf16[64,3,1,128]{3,2,1,0:T(2,128)(2,1)}, u32[]{:S(2)}, u32[]{:S(2)}) collective-permute-start(bf16[64,3,1,128]{3,2,1,0:T(2,128)(2,1)} %get-tuple-element.106), channel_id=1, source_target_pairs={{0,16},{1,17},{2,18},{3,19},{4,20},{5,21},{6,22},{7,23},{8,24},{9,... | collective-permute-start | bytes 147464 | tf_op jit(solution)/shard_map/ppermute | solution.py:18
  30.0 29.3 %collective-permute-start.1 = (bf16[64,3,1,128]{3,2,1,0:T(2,128)(2,1)}, bf16[64,3,1,128]{3,2,1,0:T(2,128)(2,1)}, u32[]{:S(2)}, u32[]{:S(2)}) collective-permute-start(bf16[64,3,1,128]{3,2,1,0:T(2,128)(2,1)} %get-tuple-element.107), channel_id=1, source_target_pairs={{16,0},{17,1},{18,2},{19,3},{20,4},{21,5},{22,6},{23,7},{24,8},{25... | collective-permute-start | bytes 147464 | tf_op jit(solution)/shard_map/ppermute | solution.py:21
  38.1 1.5 copy-start.5
  44.4 2.5 %copy-start = (f32[64,1,3,16,1]{4,3,2,0,1:T(8,128)S(1)}, f32[64,1,3,16,1]{4,3,2,0,1:T(8,128)}, u32[]{:S(2)}) copy-start(f32[64,1,3,16,1]{4,3,2,0,1:T(8,128)} %copy.30) | copy-start | bytes 36868
  46.9 7.0 %copy-start.3 = (bf16[64,3,16,128]{3,2,1,0:T(8,128)(2,1)S(1)}, bf16[64,3,16,128]{3,2,1,0:T(8,128)(2,1)}, u32[]{:S(2)}) copy-start(bf16[64,3,16,128]{3,2,1,0:T(8,128)(2,1)} %param.6) | copy-start | bytes 2359300
  60.9 1.1 copy-start.2
  62.3 1.6 copy-start.1
  65.1 1.1 copy-start.4
Sparse Core Ops, SparseCore 0:
  152.3 64.7 reduce-scatter.1
where the time goes:
time: 227 us; the launch traced here: 225 us
  waiting for transfers between devices  64.9 us (29%)
  local copies, waits for them, and re-layouts  42.5 us (19%)
  loops' own time  31.8 us (14%)
  other arithmetic  28.2 us (12%)
  matrix products  23.3 us (10%)
  between operations  13.6 us (6%)
  starting transfers between devices  10.9 us (5%)
  blocking collectives  10.3 us (5%)
    reduce_scatter x1, waiting for transfers between devices, shards(): lax.psum_scatter(arranged, ('tx', 'ty'), scatter_dimension=1, tiled=True)  64.9 us
    another operation x1, loops' own time, block_tensor(): pieces = lax.map(one_block, starts)  31.8 us
    dot_general x16, matrix products, project(): lax.dot_general(flat, basis, (((1,), (1,)), ((), ())), preferred_element_...  23.3 us
    convert_element_type x16, other arithmetic, one_block(): lax.dynamic_slice_in_dim(grads, start, width, 0).astype(jnp.float32)  15 us
    all_gather x1, blocking collectives, shards(): whole = lax.all_gather(direct_modes, 'pg', axis=0, tiled=True)  10.3 us
    dynamic_slice x16, local copies, waits for them, and re-layouts, block_tensor(): pieces = lax.map(one_block, starts)  9.31 us
    ppermute x2, starting transfers between devices, extended(): lax.ppermute(lax.slice_in_dim(block, block.shape[dim] - width, None, axis...  8.12 us
    another operation x1, other arithmetic  6.81 us
  transfers between devices with their start and end apart: 5, of which 1 were waited for; matrix products, arithmetic and copies ran while one was open for 13% of the time, Pallas kernels for 0%

commit v1 on v0

v1 whole, which is shorter than its diff:
```python
import functools
import math

import jax
import jax.numpy as jnp
from jax import lax
from jax.experimental import pallas as pl
from jax.experimental.pallas import tpu as pltpu
from jax.sharding import PartitionSpec as P

NBLK = 8
CZ = 4
MESH = pl.DeviceIdType.MESH
F32 = jnp.float32
BF16 = jnp.bfloat16


def kernel(
    tx_n, ty_n, pg_n, weight,
    order_ref, own_ref, adj_ref, out_ref,
    wide, face_lo, face_hi, edge_lo, edge_hi, us, gs, row_us, row_gs, pairs, acc, stage, parts,
    mode_send, mode_recv, x_send, x_recv, y_send, y_recv, part_send, part_recv,
):
    tx, ty, pg = lax.axis_index("tx"), lax.axis_index("ty"), lax.axis_index("pg")
    nx, _, own_n, lanes = own_ref.shape
    group_n = tx_n * ty_n
    me = tx * ty_n + ty
    rows_n = own_n
    blk = pg_n * own_n // NBLK
    per_group = NBLK // pg_n

    has_xl, has_xh = tx > 0, tx < tx_n - 1
    has_yl, has_yh = ty > 0, ty < ty_n - 1

    barrier = pltpu.get_barrier_semaphore()
    for off in range(1, pg_n):
        pl.semaphore_signal(barrier, inc=1, device_id=(tx, ty, lax.rem(pg + off, pg_n)), device_id_type=MESH)
    for off in range(1, group_n):
        to = lax.rem(me + off, group_n)
        pl.semaphore_signal(barrier, inc=1, device_id=(to // ty_n, lax.rem(to, ty_n), pg), device_id_type=MESH)
    for has, dx, dy in ((has_xl, -1, 0), (has_xh, 1, 0), (has_yl, 0, -1), (has_yh, 0, 1)):
        @pl.when(has)
        def _():
            for off in range(1, pg_n):
                pl.semaphore_signal(
                    barrier, inc=1, device_id=(tx + dx, ty + dy, lax.rem(pg + off, pg_n)), device_id_type=MESH)

    lane = lax.broadcasted_iota(jnp.int32, (own_n, lanes), 1)
    for c in range(3):
        low = jnp.zeros((own_n, lanes), F32)
        high = jnp.zeros((own_n, lanes), F32)
        for x in range(nx):
            tile = own_ref[x, c].astype(F32)
            here = (lane >= x * CZ) & (lane < (x + 1) * CZ)
            low = jnp.where(here, pltpu.roll(tile, (x * CZ) % lanes, 1) if x else tile, low)
            high = jnp.where(here, pltpu.roll(tile, (x * CZ + CZ) % lanes, 1), high)
        face_lo[c] = low.astype(BF16)
        face_hi[c] = high.astype(BF16)

    zero = jnp.zeros((pg_n, 3, own_n, lanes), BF16)

    @pl.when(jnp.logical_not(has_xl))
    def _():
        wide[0] = zero

    @pl.when(jnp.logical_not(has_xh))
    def _():
        wide[nx + 1] = zero

    @pl.when(jnp.logical_not(has_yl))
    def _():
        edge_lo[...] = zero

    @pl.when(jnp.logical_not(has_yh))
    def _():
        edge_hi[...] = zero

    neighbours = 1 * (has_xl.astype(jnp.int32) + has_xh.astype(jnp.int32)
                      + has_yl.astype(jnp.int32) + has_yh.astype(jnp.int32))
    pl.semaphore_wait(barrier, (pg_n - 1) + (group_n - 1) + neighbours * (pg_n - 1))

    def mode_copy(off):
        return pltpu.make_async_remote_copy(
            own_ref, wide.at[pl.ds(1, nx), pg], mode_send.at[off], mode_recv.at[off],
            device_id=(tx, ty, lax.rem(pg + off, pg_n)), device_id_type=MESH)

    def x_copy(side, off):
        src, dst, to = (own_ref.at[nx - 1], wide.at[0, pg], tx + 1) if side == 0 else (
            own_ref.at[0], wide.at[nx + 1, pg], tx - 1)
        return pltpu.make_async_remote_copy(
            src, dst, x_send.at[side, off], x_recv.at[side, off],
            device_id=(to, ty, lax.rem(pg + off, pg_n)), device_id_type=MESH)

    def y_copy(side, off):
        src, dst, to = (face_hi, edge_lo.at[pg], ty + 1) if side == 0 else (face_lo, edge_hi.at[pg], ty - 1)
        return pltpu.make_async_remote_copy(
            src, dst, y_send.at[side, off], y_recv.at[side, off],
            device_id=(tx, to, lax.rem(pg + off, pg_n)), device_id_type=MESH)

    sides = ((x_copy, 0, has_xh, has_xl), (x_copy, 1, has_xl, has_xh),
             (y_copy, 0, has_yh, has_yl), (y_copy, 1, has_yl, has_yh))
    for off in range(1, pg_n):
        mode_copy(off).start()
    for copy, side, sends, _ in sides:
        @pl.when(sends)
        def _():
            for off in range(pg_n):
                copy(side, off).start()
    wide[pl.ds(1, nx), pg] = own_ref[...]
    acc[...] = jnp.zeros_like(acc)
    for off in range(1, pg_n):
        mode_copy(off).wait()
    for copy, side, sends, gets in sides:
        @pl.when(sends)
        def _():
            for off in range(pg_n):
                copy(side, off).wait_send()

        @pl.when(gets)
        def _():
            for off in range(pg_n):
                copy(side, off).wait_recv()

    place = lax.rem(lane, CZ)
    chunk_j = 256 // rows_n
    chunks = pg_n * own_n // chunk_j

    def grads(x, xx):
        for p in range(pg_n):
            rows = pl.ds(p * own_n // blk, own_n // blk)
            for c in range(3):
                u = wide[x + 1, p, c].astype(F32)
                us[xx, c, rows] = u.reshape(own_n // blk, blk, lanes)
                gx = wide[x + 2, p, c].astype(F32) - wide[x, p, c].astype(F32)
                e_hi = pltpu.roll(edge_hi[p, c].astype(F32), lanes - CZ - x * CZ, 1)
                e_lo = pltpu.roll(edge_lo[p, c].astype(F32), lax.rem(lanes - x * CZ, lanes), 1)
                up = jnp.where(lane >= lanes - CZ, e_hi, pltpu.roll(u, lanes - CZ, 1))
                down = jnp.where(lane < CZ, e_lo, pltpu.roll(u, CZ, 1))
                gy = up - down
                upper = jnp.where(place == CZ - 1, pltpu.roll(u, CZ - 1, 1), pltpu.roll(u, lanes - 1, 1))
                lower = jnp.where(place == 0, pltpu.roll(u, lanes - CZ + 1, 1), pltpu.roll(u, 1, 1))
                gz = upper - lower
                for d, g in enumerate((gx, gy, gz)):
                    g = (g * 0.5).astype(BF16).astype(F32)
                    gs[xx, d * 3 + c, rows] = g.reshape(own_n // blk, blk, lanes)

    def step(xp, carry):
        for xx in range(2):
            grads(xp * 2 + xx, xx)
            for b in range(per_group):
                s = order_ref[pg * per_group + b]
                for d in range(3):
                    row_us[xx, d, b] = us[xx, d, s]
                for i in range(9):
                    row_gs[xx, i, b] = gs[xx, i, s]

        def one_chunk(ch, carry):
            for xx in range(2):
                row_u = [[row_us[xx, d, b] for b in range(per_group)] for d in range(3)]
                row_g = [[row_gs[xx, i, b] for b in range(per_group)] for i in range(9)]
                for jj in range(chunk_j):
                    jb, jr = ch * (chunk_j // blk) + jj // blk, pl.ds(jj % blk, 1)
                    ju = [jnp.broadcast_to(us[xx, d, jb, jr], (blk, lanes)) for d in range(3)]
                    jg = [jnp.broadcast_to(gs[xx, i, jb, jr], (blk, lanes)) for i in range(9)]
                    for c in range(3):
                        both = []
                        for b in range(per_group):
                            total = row_u[0][b] * jg[c] + ju[0] * row_g[c][b]
                            for d in range(1, 3):
                                total = total + row_u[d][b] * jg[d * 3 + c]
                                total = total + ju[d] * row_g[d * 3 + c][b]
                            both.append(total)
                        pairs[c, pl.ds(jj * rows_n, rows_n), pl.ds(xx * lanes, lanes)] = (
                            jnp.concatenate(both, 0).astype(BF16))
            total = acc[ch]
            for c in range(3):
                basis = jnp.concatenate([adj_ref[c, xp * 2], adj_ref[c, xp * 2 + 1]], 1)
                total = total + lax.dot_general(
                    basis, pairs[c], (((1,), (1,)), ((), ())), preferred_element_type=F32)
            acc[ch] = total
            return carry

        return lax.fori_loop(0, chunks, one_chunk, carry)

    lax.fori_loop(0, nx // 2, step, 0)

    _, _, k_width, width = stage.shape
    for q in range(ty_n):
        first = q * width
        block = acc[first // 256] * weight
        for t in range(tx_n):
            stage[q, t] = block[t * k_width:(t + 1) * k_width, first % 256:first % 256 + width].astype(stage.dtype)

    def part_copy(off):
        to = lax.rem(me + off, group_n)
        to_x, to_y = to // ty_n, lax.rem(to, ty_n)
        return pltpu.make_async_remote_copy(
            stage.at[to_y, to_x], parts.at[me], part_send.at[off], part_recv.at[off],
            device_id=(to_x, to_y, pg), device_id_type=MESH)

    for off in range(1, group_n):
        part_copy(off).start()
    parts[me] = stage[ty, tx]
    for off in range(1, group_n):
        part_copy(off).wait()
    result = parts[0].astype(F32)
    for source in range(1, group_n):
        result = result + parts[source].astype(F32)
    out_ref[...] = result


def shards(direct_modes, adjoint_modes, block_order):
    tx_n, ty_n, pg_n = lax.axis_size("tx"), lax.axis_size("ty"), lax.axis_size("pg")
    own_n, _, nx, lanes = direct_modes.shape
    adj_n = adjoint_modes.shape[0]
    mode_n = own_n * pg_n
    weight = 1.0 / math.sqrt(3.0 * nx * tx_n * lanes * ty_n)
    j_width, k_width = mode_n // ty_n, adj_n // tx_n
    width = j_width * own_n
    blk = mode_n // NBLK
    own = jnp.transpose(direct_modes, (2, 1, 0, 3))
    adj = jnp.transpose(adjoint_modes, (1, 2, 0, 3))
    vmem = pl.BlockSpec(memory_space=pltpu.VMEM)
    dma = pltpu.SemaphoreType.DMA
    summed = pl.pallas_call(
        functools.partial(kernel, tx_n, ty_n, pg_n, weight),
        out_shape=jax.ShapeDtypeStruct((k_width, width), F32),
        in_specs=[pl.BlockSpec(memory_space=pltpu.SMEM), vmem, vmem],
        out_specs=vmem,
        scratch_shapes=[
            pltpu.VMEM((nx + 2, pg_n, 3, own_n, lanes), BF16),
            pltpu.VMEM((3, own_n, lanes), BF16),
            pltpu.VMEM((3, own_n, lanes), BF16),
            pltpu.VMEM((pg_n, 3, own_n, lanes), BF16),
            pltpu.VMEM((pg_n, 3, own_n, lanes), BF16),
            pltpu.VMEM((2, 3, NBLK, blk, lanes), F32),
            pltpu.VMEM((2, 9, NBLK, blk, lanes), F32),
            pltpu.VMEM((2, 3, NBLK // pg_n, blk, lanes), F32),
            pltpu.VMEM((2, 9, NBLK // pg_n, blk, lanes), F32),
            pltpu.VMEM((3, 256, 2 * lanes), BF16),
            pltpu.VMEM((mode_n * own_n // 256, adj_n, 256), F32),
            pltpu.VMEM((ty_n, tx_n, k_width, width), BF16),
            pltpu.VMEM((tx_n * ty_n, k_width, width), BF16),
            dma((pg_n,)), dma((pg_n,)),
            dma((2, pg_n)), dma((2, pg_n)),
            dma((2, pg_n)), dma((2, pg_n)),
            dma((tx_n * ty_n,)), dma((tx_n * ty_n,)),
        ],
        compiler_params=pltpu.CompilerParams(
            collective_id=0, has_side_effects=True, vmem_limit_bytes=40 * 2**20),
    )(block_order, own, adj)
    return jnp.transpose(summed.reshape(k_width, j_width, own_n), (2, 1, 0))


def solution(mesh):
    placed = (P("pg", None, "tx", "ty"), P(None, None, "tx", "ty"), P())
    return jax.shard_map(
        shards, mesh=mesh, in_specs=placed, out_specs=P("pg", "ty", "tx"), check_vma=False
    )
```

time: 227 us -> 45.9 us (0.20)
  waiting for transfers between devices: 64.9 us -> 0 us
  Pallas kernels: 0 us -> 41.9 us
  local copies, waits for them, and re-layouts: 42.5 us -> 3.77 us
  loops' own time: 31.8 us -> 0 us
  other arithmetic: 28.2 us -> 0 us
  matrix products: 23.3 us -> 0 us
  between operations: 13.6 us -> 0.02 us
  starting transfers between devices: 10.9 us -> 0 us
  blocking collectives: 10.3 us -> 0 us
    reduce_scatter x1 -> x0, waiting for transfers between devices: 64.9 us -> none  [shards(): lax.psum_scatter(arranged, ('tx', 'ty'), scatter_dimension=1, tiled=True)]
    pallas_call x0 -> x1, Pallas kernels: none -> 41.9 us  [shards(): pl.pallas_call(functools.partial(kernel, tx_n, ty_n, pg_n, weight), out_s...]
    another operation x1 -> x0, loops' own time: 31.8 us -> none  [block_tensor(): pieces = lax.map(one_block, starts)]
    dot_general x16 -> x0, matrix products: 23.3 us -> none  [project(): lax.dot_general(flat, basis, (((1,), (1,)), ((), ())), preferred_element_...]
    convert_element_type x37 -> x0, other arithmetic: 19.1 us -> none  [the longest x16 15 us: one_block(): lax.dynamic_slice_in_dim(grads, start, width, 0).astype(jnp.float32)]
    ppermute x4 -> x0, starting transfers between devices: 10.9 us -> none  [the longest x2 8.12 us: extended(): lax.ppermute(lax.slice_in_dim(block, block.shape[dim] - width, None, axis...]
    all_gather x1 -> x0, blocking collectives: 10.3 us -> none  [shards(): whole = lax.all_gather(direct_modes, 'pg', axis=0, tiled=True)]
    concatenate x5 -> x0, local copies, waits for them, and re-layouts: 10.1 us -> none  [the longest x2 4.34 us: depth_slope(): jnp.roll(values, 1 - depth, -1)]
  transfers between devices with their start and end apart: 5 -> 0, of which waited for: 1 -> 0; matrix products, arithmetic and copies ran while one was open for 13% -> 0% of each run, Pallas kernels for 0% -> 0%
where the time goes in v1:
time: 45.9 us; the launch traced here: 45.7 us
  Pallas kernels  41.9 us (91%)
  local copies, waits for them, and re-layouts  3.77 us (8%)
    pallas_call x1, Pallas kernels, shards(): pl.pallas_call(functools.partial(kernel, tx_n, ty_n, pg_n, weight), out_s...  41.9 us
    unnamed x4, local copies, waits for them, and re-layouts  2.97 us

profile of v1, /device:TPU:0, one launch (start us, length us, event | category | flops | bytes accessed | tf_op | source)
XLA Modules:
  0.0 45.7 jit_solution(3129680434579656058)
XLA Ops:
  0.0 1.0 %copy.14 = bf16[16,3,16,128]{3,0,1,2:T(8,128)(2,1)S(1)} copy(bf16[16,3,16,128]{3,2,1,0:T(8,128)(2,1)} %param.3) | data formatting | bytes 393216 | tf_op args[0]
  1.0 1.3 %copy.13 = bf16[64,3,16,128]{3,0,2,1:T(8,128)(2,1)S(1)} copy(bf16[64,3,16,128]{3,2,1,0:T(8,128)(2,1)} %param.4) | data formatting | bytes 1572864 | tf_op args[1]
  2.3 0.0 copy-start
  2.3 0.6 %copy-done = s32[8]{0:T(128)S(1)} copy-done((s32[8]{0:T(128)S(1)}, s32[8]{0:T(128)}, u32[]{:S(2)}) %copy-start) | copy-done | bytes 56
  3.0 41.9 %shard_map.37 = f32[32,256]{1,0:T(8,128)S(1)} custom-call(s32[8]{0:T(128)S(1)} %copy-done, bf16[16,3,16,128]{3,2,1,0:T(8,128)(2,1)S(1)} %bitcast.10, bf16[3,16,64,128]{3,2,1,0:T(8,128)(2,1)S(1)} %bitcast.9), custom_call_target="tpu_custom_call" | custom-call | tf_op jit(solution)/shard_map/pallas_call | solution.py:225
  44.9 0.1 copy.9
  45.0 0.7 %copy.10 = f32[16,16,32]{2,1,0:T(8,128)} copy(f32[16,16,32]{2,0,1:T(8,128)S(1)} %bitcast.11) | data formatting | bytes 65536 | tf_op jit(solution)/shard_map/transpose | solution.py:252
Async XLA Ops:
  2.3 0.7 %copy-start = (s32[8]{0:T(128)S(1)}, s32[8]{0:T(128)}, u32[]{:S(2)}) copy-start(s32[8]{0:T(128)} %order_ref.1) | copy-start | bytes 100

commit v2 on v1

--- a/solution.py
+++ b/solution.py
@@ -10,6 +10,7 @@
 
 NBLK = 8
 CZ = 4
+QUARTERS = 4
 MESH = pl.DeviceIdType.MESH
 F32 = jnp.float32
 BF16 = jnp.bfloat16
@@ -18,7 +19,7 @@
 def kernel(
     tx_n, ty_n, pg_n, weight,
     order_ref, own_ref, adj_ref, out_ref,
-    wide, face_lo, face_hi, edge_lo, edge_hi, us, gs, row_us, row_gs, pairs, acc, stage, parts,
+    wide, face_lo, face_hi, edge_lo, edge_hi, us, gs, row_us, row_gs, pairs_a, pairs_b, acc, stage, parts,
     mode_send, mode_recv, x_send, x_recv, y_send, y_recv, part_send, part_recv,
 ):
     tx, ty, pg = lax.axis_index("tx"), lax.axis_index("ty"), lax.axis_index("pg")
@@ -26,6 +27,7 @@
     group_n = tx_n * ty_n
     me = tx * ty_n + ty
     rows_n = own_n
+    quarter = nx // QUARTERS
     blk = pg_n * own_n // NBLK
     per_group = NBLK // pg_n
 
@@ -79,9 +81,10 @@
                       + has_yl.astype(jnp.int32) + has_yh.astype(jnp.int32))
     pl.semaphore_wait(barrier, (pg_n - 1) + (group_n - 1) + neighbours * (pg_n - 1))
 
-    def mode_copy(off):
+    def mode_copy(off, q):
         return pltpu.make_async_remote_copy(
-            own_ref, wide.at[pl.ds(1, nx), pg], mode_send.at[off], mode_recv.at[off],
+            own_ref.at[pl.ds(q * quarter, quarter)], wide.at[pl.ds(1 + q * quarter, quarter), pg],
+            mode_send.at[off, q], mode_recv.at[off, q],
             device_id=(tx, ty, lax.rem(pg + off, pg_n)), device_id_type=MESH)
 
     def x_copy(side, off):
@@ -99,38 +102,40 @@
 
     sides = ((x_copy, 0, has_xh, has_xl), (x_copy, 1, has_xl, has_xh),
              (y_copy, 0, has_yh, has_yl), (y_copy, 1, has_yl, has_yh))
-    for off in range(1, pg_n):
-        mode_copy(off).start()
     for copy, side, sends, _ in sides:
         @pl.when(sends)
         def _():
             for off in range(pg_n):
                 copy(side, off).start()
+    for q in range(QUARTERS):
+        for off in range(1, pg_n):
+            mode_copy(off, q).start()
     wide[pl.ds(1, nx), pg] = own_ref[...]
-    acc[...] = jnp.zeros_like(acc)
+    pairs_b[...] = jnp.zeros_like(pairs_b)
+
+    def arrived(sides):
+        for copy, side, _, gets in sides:
+            @pl.when(gets)
+            def _():
+                for off in range(pg_n):
+                    copy(side, off).wait_recv()
+
+    arrived((sides[0], sides[2], sides[3]))
     for off in range(1, pg_n):
-        mode_copy(off).wait()
-    for copy, side, sends, gets in sides:
-        @pl.when(sends)
-        def _():
-            for off in range(pg_n):
-                copy(side, off).wait_send()
-
-        @pl.when(gets)
-        def _():
-            for off in range(pg_n):
-                copy(side, off).wait_recv()
+        mode_copy(off, 0).wait_recv()
 
     place = lax.rem(lane, CZ)
     chunk_j = 256 // rows_n
     chunks = pg_n * own_n // chunk_j
-
-    def grads(x, xx):
+    per_chunk = ty_n // chunks
+    _, _, k_width, width = stage.shape
+
+    def grads(x, carry):
         for p in range(pg_n):
             rows = pl.ds(p * own_n // blk, own_n // blk)
             for c in range(3):
                 u = wide[x + 1, p, c].astype(F32)
-                us[xx, c, rows] = u.reshape(own_n // blk, blk, lanes)
+                us[x, c, rows] = u.reshape(own_n // blk, blk, lanes)
                 gx = wide[x + 2, p, c].astype(F32) - wide[x, p, c].astype(F32)
                 e_hi = pltpu.roll(edge_hi[p, c].astype(F32), lanes - CZ - x * CZ, 1)
                 e_lo = pltpu.roll(edge_lo[p, c].astype(F32), lax.rem(lanes - x * CZ, lanes), 1)
@@ -142,54 +147,39 @@
                 gz = upper - lower
                 for d, g in enumerate((gx, gy, gz)):
                     g = (g * 0.5).astype(BF16).astype(F32)
-                    gs[xx, d * 3 + c, rows] = g.reshape(own_n // blk, blk, lanes)
-
-    def step(xp, carry):
+                    gs[x, d * 3 + c, rows] = g.reshape(own_n // blk, blk, lanes)
+        for b in range(per_group):
+            s = order_ref[pg * per_group + b]
+            for d in range(3):
+                row_us[x, d, b] = us[x, d, s]
+            for i in range(9):
+                row_gs[x, i, b] = gs[x, i, s]
+        return carry
+
+    def form(pairs, x0, ch):
         for xx in range(2):
-            grads(xp * 2 + xx, xx)
-            for b in range(per_group):
-                s = order_ref[pg * per_group + b]
-                for d in range(3):
-                    row_us[xx, d, b] = us[xx, d, s]
-                for i in range(9):
-                    row_gs[xx, i, b] = gs[xx, i, s]
-
-        def one_chunk(ch, carry):
-            for xx in range(2):
-                row_u = [[row_us[xx, d, b] for b in range(per_group)] for d in range(3)]
-                row_g = [[row_gs[xx, i, b] for b in range(per_group)] for i in range(9)]
-                for jj in range(chunk_j):
-                    jb, jr = ch * (chunk_j // blk) + jj // blk, pl.ds(jj % blk, 1)
-                    ju = [jnp.broadcast_to(us[xx, d, jb, jr], (blk, lanes)) for d in range(3)]
-                    jg = [jnp.broadcast_to(gs[xx, i, jb, jr], (blk, lanes)) for i in range(9)]
-                    for c in range(3):
-                        both = []
-                        for b in range(per_group):
-                            total = row_u[0][b] * jg[c] + ju[0] * row_g[c][b]
-                            for d in range(1, 3):
-                                total = total + row_u[d][b] * jg[d * 3 + c]
-                                total = total + ju[d] * row_g[d * 3 + c][b]
-                            both.append(total)
-                        pairs[c, pl.ds(jj * rows_n, rows_n), pl.ds(xx * lanes, lanes)] = (
-                            jnp.concatenate(both, 0).astype(BF16))
-            total = acc[ch]
-            for c in range(3):
-                basis = jnp.concatenate([adj_ref[c, xp * 2], adj_ref[c, xp * 2 + 1]], 1)
-                total = total + lax.dot_general(
-                    basis, pairs[c], (((1,), (1,)), ((), ())), preferred_element_type=F32)
-            acc[ch] = total
-            return carry
-
-        return lax.fori_loop(0, chunks, one_chunk, carry)
-
-    lax.fori_loop(0, nx // 2, step, 0)
-
-    _, _, k_width, width = stage.shape
-    for q in range(ty_n):
-        first = q * width
-        block = acc[first // 256] * weight
-        for t in range(tx_n):
-            stage[q, t] = block[t * k_width:(t + 1) * k_width, first % 256:first % 256 + width].astype(stage.dtype)
+            x = x0 + xx
+            row_u = [[row_us[x, d, b] for b in range(per_group)] for d in range(3)]
+            row_g = [[row_gs[x, i, b] for b in range(per_group)] for i in range(9)]
+            for jj in range(chunk_j):
+                jb, jr = ch * (chunk_j // blk) + jj // blk, pl.ds(jj % blk, 1)
+                ju = [jnp.broadcast_to(us[x, d, jb, jr], (blk, lanes)) for d in range(3)]
+                jg = [jnp.broadcast_to(gs[x, i, jb, jr], (blk, lanes)) for i in range(9)]
+                for c in range(3):
+                    both = []
+                    for b in range(per_group):
+                        total = row_u[0][b] * jg[c] + ju[0] * row_g[c][b]
+                        for d in range(1, 3):
+                            total = total + row_u[d][b] * jg[d * 3 + c]
+                            total = total + ju[d] * row_g[d * 3 + c][b]
+                        both.append(total)
+                    pairs[pl.ds(jj * rows_n, rows_n), pl.ds((2 * c + xx) * lanes, lanes)] = (
+                        jnp.concatenate(both, 0).astype(BF16))
+
+    def projected(pairs, x0):
+        basis = jnp.concatenate([adj_ref[c, x0 + xx] for c in range(3) for xx in range(2)], 1)
+        return lax.dot_general(
+            basis, pairs[...], (((1,), (1,)), ((), ())), preferred_element_type=F32)
 
     def part_copy(off):
         to = lax.rem(me + off, group_n)
@@ -198,9 +188,63 @@
             stage.at[to_y, to_x], parts.at[me], part_send.at[off], part_recv.at[off],
             device_id=(to_x, to_y, pg), device_id_type=MESH)
 
-    for off in range(1, group_n):
-        part_copy(off).start()
+    def step(index, carry):
+        turn, q = index // QUARTERS, lax.rem(index, QUARTERS)
+        ch = lax.rem(ty // per_chunk + 1 + turn, chunks)
+
+        @pl.when(turn == 0)
+        def _():
+            @pl.when(q < QUARTERS - 1)
+            def _():
+                for off in range(1, pg_n):
+                    mode_copy(off, q + 1).wait_recv()
+
+            @pl.when(q == QUARTERS - 1)
+            def _():
+                arrived((sides[1],))
+
+            lax.fori_loop(q * quarter, (q + 1) * quarter, grads, 0)
+
+        def two(i, carry):
+            x0 = q * quarter + 4 * i
+            form(pairs_a, x0, ch)
+            before = acc[...] + projected(pairs_b, lax.rem(x0 + nx - 2, nx))
+            acc[...] = jnp.where(x0 == 0, 0.0, before)
+            form(pairs_b, x0 + 2, ch)
+            acc[...] += projected(pairs_a, x0)
+            return carry
+
+        if quarter == 4:
+            two(0, 0)
+        else:
+            lax.fori_loop(0, quarter // 4, two, 0)
+
+        @pl.when(q == QUARTERS - 1)
+        def _():
+            block = (acc[...] + projected(pairs_b, nx - 2)) * weight
+            for i in range(per_chunk):
+                to_y = ch * per_chunk + i
+                for t in range(tx_n):
+                    stage[to_y, t] = block[
+                        t * k_width:(t + 1) * k_width, i * width:(i + 1) * width].astype(stage.dtype)
+                    to = t * ty_n + to_y
+
+                    @pl.when(to != me)
+                    def _():
+                        part_copy(lax.rem(to - me + group_n, group_n)).start()
+        return carry
+
+    lax.fori_loop(0, chunks * QUARTERS, step, 0)
     parts[me] = stage[ty, tx]
+
+    for q in range(QUARTERS):
+        for off in range(1, pg_n):
+            mode_copy(off, q).wait_send()
+    for copy, side, sends, _ in sides:
+        @pl.when(sends)
+        def _():
+            for off in range(pg_n):
+                copy(side, off).wait_send()
     for off in range(1, group_n):
         part_copy(off).wait()
     result = parts[0].astype(F32)
@@ -233,15 +277,16 @@
             pltpu.VMEM((3, own_n, lanes), BF16),
             pltpu.VMEM((pg_n, 3, own_n, lanes), BF16),
             pltpu.VMEM((pg_n, 3, own_n, lanes), BF16),
-            pltpu.VMEM((2, 3, NBLK, blk, lanes), F32),
-            pltpu.VMEM((2, 9, NBLK, blk, lanes), F32),
-            pltpu.VMEM((2, 3, NBLK // pg_n, blk, lanes), F32),
-            pltpu.VMEM((2, 9, NBLK // pg_n, blk, lanes), F32),
-            pltpu.VMEM((3, 256, 2 * lanes), BF16),
-            pltpu.VMEM((mode_n * own_n // 256, adj_n, 256), F32),
+            pltpu.VMEM((nx, 3, NBLK, blk, lanes), F32),
+            pltpu.VMEM((nx, 9, NBLK, blk, lanes), F32),
+            pltpu.VMEM((nx, 3, NBLK // pg_n, blk, lanes), F32),
+            pltpu.VMEM((nx, 9, NBLK // pg_n, blk, lanes), F32),
+            pltpu.VMEM((256, 6 * lanes), BF16),
+            pltpu.VMEM((256, 6 * lanes), BF16),
+            pltpu.VMEM((adj_n, 256), F32),
             pltpu.VMEM((ty_n, tx_n, k_width, width), BF16),
             pltpu.VMEM((tx_n * ty_n, k_width, width), BF16),
-            dma((pg_n,)), dma((pg_n,)),
+            dma((pg_n, QUARTERS)), dma((pg_n, QUARTERS)),
             dma((2, pg_n)), dma((2, pg_n)),
             dma((2, pg_n)), dma((2, pg_n)),
             dma((tx_n * ty_n,)), dma((tx_n * ty_n,)),

time: 45.9 us -> 40.6 us (0.88)
  Pallas kernels: 41.9 us -> 36.6 us
    pallas_call x1, Pallas kernels: 41.9 us -> 36.6 us  [shards(): pl.pallas_call(functools.partial(kernel, tx_n, ty_n, pg_n, weight), out_s...]
where the time goes in v2:
time: 40.6 us; the launch traced here: 40.4 us
  Pallas kernels  36.6 us (90%)
  local copies, waits for them, and re-layouts  3.77 us (9%)
    pallas_call x1, Pallas kernels, shards(): pl.pallas_call(functools.partial(kernel, tx_n, ty_n, pg_n, weight), out_s...  36.6 us
    unnamed x4, local copies, waits for them, and re-layouts  2.97 us

profile of v2, /device:TPU:0, one launch (start us, length us, event | category | flops | bytes accessed | tf_op | source)
XLA Modules:
  0.0 40.4 jit_solution(5268101143626251860)
XLA Ops:
  0.0 1.0 %copy.14 = bf16[16,3,16,128]{3,0,1,2:T(8,128)(2,1)S(1)} copy(bf16[16,3,16,128]{3,2,1,0:T(8,128)(2,1)} %param.3) | data formatting | bytes 393216 | tf_op args[0]
  1.0 1.3 %copy.13 = bf16[64,3,16,128]{3,0,2,1:T(8,128)(2,1)S(1)} copy(bf16[64,3,16,128]{3,2,1,0:T(8,128)(2,1)} %param.4) | data formatting | bytes 1572864 | tf_op args[1]
  2.3 0.0 copy-start
  2.3 0.6 %copy-done = s32[8]{0:T(128)S(1)} copy-done((s32[8]{0:T(128)S(1)}, s32[8]{0:T(128)}, u32[]{:S(2)}) %copy-start) | copy-done | bytes 56
  3.0 36.6 %shard_map.37 = f32[32,256]{1,0:T(8,128)S(1)} custom-call(s32[8]{0:T(128)S(1)} %copy-done, bf16[16,3,16,128]{3,2,1,0:T(8,128)(2,1)S(1)} %bitcast.10, bf16[3,16,64,128]{3,2,1,0:T(8,128)(2,1)S(1)} %bitcast.9), custom_call_target="tpu_custom_call" | custom-call | tf_op jit(solution)/shard_map/pallas_call | solution.py:269
  39.6 0.1 copy.9
  39.7 0.7 %copy.10 = f32[16,16,32]{2,1,0:T(8,128)} copy(f32[16,16,32]{2,0,1:T(8,128)S(1)} %bitcast.11) | data formatting | bytes 65536 | tf_op jit(solution)/shard_map/transpose | solution.py:297
Async XLA Ops:
  2.3 0.7 %copy-start = (s32[8]{0:T(128)S(1)}, s32[8]{0:T(128)}, u32[]{:S(2)}) copy-start(s32[8]{0:T(128)} %order_ref.1) | copy-start | bytes 100

commit v3 on v2

--- a/solution.py
+++ b/solution.py
@@ -11,6 +11,8 @@
 NBLK = 8
 CZ = 4
 QUARTERS = 4
+CHUNK = 512
+PIECES = 1
 MESH = pl.DeviceIdType.MESH
 F32 = jnp.float32
 BF16 = jnp.bfloat16
@@ -18,12 +20,17 @@
 
 def kernel(
     tx_n, ty_n, pg_n, weight,
-    order_ref, own_ref, adj_ref, out_ref,
-    wide, face_lo, face_hi, edge_lo, edge_hi, us, gs, row_us, row_gs, pairs_a, pairs_b, acc, stage, parts,
+    order_ref, own_any, adj_in, out_ref,
+    own_in, own_sem, own_flat, own_ref, adj_raw, adj_flat, adj_sem, wide, face_lo, face_hi, edge_lo, edge_hi, us, gs, row_us, row_gs, pairs_a, pairs_b, acc, stage, parts,
     mode_send, mode_recv, x_send, x_recv, y_send, y_recv, part_send, part_recv,
 ):
     tx, ty, pg = lax.axis_index("tx"), lax.axis_index("ty"), lax.axis_index("pg")
     nx, _, own_n, lanes = own_ref.shape
+    adj_n = adj_raw.shape[0]
+    own_copy = pltpu.make_async_copy(own_any, own_in, own_sem)
+    own_copy.start()
+    adj_copy = pltpu.make_async_copy(adj_in, adj_raw, adj_sem)
+    adj_copy.start()
     group_n = tx_n * ty_n
     me = tx * ty_n + ty
     rows_n = own_n
@@ -46,6 +53,14 @@
             for off in range(1, pg_n):
                 pl.semaphore_signal(
                     barrier, inc=1, device_id=(tx + dx, ty + dy, lax.rem(pg + off, pg_n)), device_id_type=MESH)
+
+    own_copy.wait()
+    for m in range(own_n):
+        for c in range(3):
+            own_flat[pl.ds(c * own_n + m, nx, stride=3 * own_n), :] = own_in[m, c].astype(F32)
+    for x in range(nx):
+        for c in range(3):
+            own_ref[x, c] = own_flat[pl.ds((x * 3 + c) * own_n, own_n), :].astype(BF16)
 
     lane = lax.broadcasted_iota(jnp.int32, (own_n, lanes), 1)
     for c in range(3):
@@ -112,6 +127,16 @@
             mode_copy(off, q).start()
     wide[pl.ds(1, nx), pg] = own_ref[...]
     pairs_b[...] = jnp.zeros_like(pairs_b)
+    adj_copy.wait()
+
+    def turn_basis(i, carry):
+        for more in range(4):
+            k = i * 4 + more
+            for c in range(3):
+                adj_flat[pl.ds(c * nx * adj_n + k, nx, stride=adj_n), :] = adj_raw[k, c].astype(F32)
+        return carry
+
+    lax.fori_loop(0, adj_n // 4, turn_basis, 0)
 
     def arrived(sides):
         for copy, side, _, gets in sides:
@@ -125,7 +150,7 @@
         mode_copy(off, 0).wait_recv()
 
     place = lax.rem(lane, CZ)
-    chunk_j = 256 // rows_n
+    chunk_j = CHUNK // rows_n
     chunks = pg_n * own_n // chunk_j
     per_chunk = ty_n // chunks
     _, _, k_width, width = stage.shape
@@ -156,12 +181,27 @@
                 row_gs[x, i, b] = gs[x, i, s]
         return carry
 
-    def form(pairs, x0, ch):
+    def projected(pairs, x0, piece=None):
+        parts_of = 6 // PIECES
+        ks = range(6) if piece is None else range(piece * parts_of, (piece + 1) * parts_of)
+        basis = jnp.concatenate(
+            [adj_flat[pl.ds(pl.multiple_of((k // 2 * nx + x0 + k % 2) * adj_n, adj_n), adj_n), :]
+             for k in ks], 1).astype(BF16)
+        return lax.dot_general(
+            basis, pairs[:, ks[0] * lanes:(ks[-1] + 1) * lanes], (((1,), (1,)), ((), ())),
+            preferred_element_type=F32)
+
+    def form(pairs, x0, ch, other, y0):
+        made = jnp.zeros((adj_n, CHUNK), F32)
         for xx in range(2):
             x = x0 + xx
             row_u = [[row_us[x, d, b] for b in range(per_group)] for d in range(3)]
             row_g = [[row_gs[x, i, b] for b in range(per_group)] for i in range(9)]
             for jj in range(chunk_j):
+                at = xx * chunk_j + jj
+                for piece in range(PIECES):
+                    if at == piece * 2 * chunk_j // PIECES:
+                        made = made + projected(other, y0, piece)
                 jb, jr = ch * (chunk_j // blk) + jj // blk, pl.ds(jj % blk, 1)
                 ju = [jnp.broadcast_to(us[x, d, jb, jr], (blk, lanes)) for d in range(3)]
                 jg = [jnp.broadcast_to(gs[x, i, jb, jr], (blk, lanes)) for i in range(9)]
@@ -175,11 +215,7 @@
                         both.append(total)
                     pairs[pl.ds(jj * rows_n, rows_n), pl.ds((2 * c + xx) * lanes, lanes)] = (
                         jnp.concatenate(both, 0).astype(BF16))
-
-    def projected(pairs, x0):
-        basis = jnp.concatenate([adj_ref[c, x0 + xx] for c in range(3) for xx in range(2)], 1)
-        return lax.dot_general(
-            basis, pairs[...], (((1,), (1,)), ((), ())), preferred_element_type=F32)
+        return made
 
     def part_copy(off):
         to = lax.rem(me + off, group_n)
@@ -207,11 +243,9 @@
 
         def two(i, carry):
             x0 = q * quarter + 4 * i
-            form(pairs_a, x0, ch)
-            before = acc[...] + projected(pairs_b, lax.rem(x0 + nx - 2, nx))
-            acc[...] = jnp.where(x0 == 0, 0.0, before)
-            form(pairs_b, x0 + 2, ch)
-            acc[...] += projected(pairs_a, x0)
+            last = form(pairs_a, x0, ch, pairs_b, lax.rem(x0 + nx - 2, nx))
+            acc[...] = jnp.where(x0 == 0, 0.0, acc[...] + last)
+            acc[...] += form(pairs_b, x0 + 2, ch, pairs_a, x0)
             return carry
 
         if quarter == 4:
@@ -262,16 +296,21 @@
     j_width, k_width = mode_n // ty_n, adj_n // tx_n
     width = j_width * own_n
     blk = mode_n // NBLK
-    own = jnp.transpose(direct_modes, (2, 1, 0, 3))
-    adj = jnp.transpose(adjoint_modes, (1, 2, 0, 3))
     vmem = pl.BlockSpec(memory_space=pltpu.VMEM)
     dma = pltpu.SemaphoreType.DMA
     summed = pl.pallas_call(
         functools.partial(kernel, tx_n, ty_n, pg_n, weight),
         out_shape=jax.ShapeDtypeStruct((k_width, width), F32),
-        in_specs=[pl.BlockSpec(memory_space=pltpu.SMEM), vmem, vmem],
+        in_specs=[pl.BlockSpec(memory_space=pltpu.SMEM)] + [pl.BlockSpec(memory_space=pl.ANY)] * 2,
         out_specs=vmem,
         scratch_shapes=[
+            pltpu.VMEM((own_n, 3, nx, lanes), BF16),
+            dma,
+            pltpu.VMEM((nx * 3 * own_n, lanes), F32),
+            pltpu.VMEM((nx, 3, own_n, lanes), BF16),
+            pltpu.VMEM((adj_n, 3, nx, lanes), BF16),
+            pltpu.VMEM((3 * nx * adj_n, lanes), F32),
+            dma,
             pltpu.VMEM((nx + 2, pg_n, 3, own_n, lanes), BF16),
             pltpu.VMEM((3, own_n, lanes), BF16),
             pltpu.VMEM((3, own_n, lanes), BF16),
@@ -281,9 +320,9 @@
             pltpu.VMEM((nx, 9, NBLK, blk, lanes), F32),
             pltpu.VMEM((nx, 3, NBLK // pg_n, blk, lanes), F32),
             pltpu.VMEM((nx, 9, NBLK // pg_n, blk, lanes), F32),
-            pltpu.VMEM((256, 6 * lanes), BF16),
-            pltpu.VMEM((256, 6 * lanes), BF16),
-            pltpu.VMEM((adj_n, 256), F32),
+            pltpu.VMEM((CHUNK, 6 * lanes), BF16),
+            pltpu.VMEM((CHUNK, 6 * lanes), BF16),
+            pltpu.VMEM((adj_n, CHUNK), F32),
             pltpu.VMEM((ty_n, tx_n, k_width, width), BF16),
             pltpu.VMEM((tx_n * ty_n, k_width, width), BF16),
             dma((pg_n, QUARTERS)), dma((pg_n, QUARTERS)),
@@ -292,8 +331,8 @@
             dma((tx_n * ty_n,)), dma((tx_n * ty_n,)),
         ],
         compiler_params=pltpu.CompilerParams(
-            collective_id=0, has_side_effects=True, vmem_limit_bytes=40 * 2**20),
-    )(block_order, own, adj)
+            collective_id=0, has_side_effects=True, vmem_limit_bytes=60 * 2**20),
+    )(block_order, direct_modes, adjoint_modes)
     return jnp.transpose(summed.reshape(k_width, j_width, own_n), (2, 1, 0))
 
 

time: 40.6 us -> 37.1 us (0.914)
  local copies, waits for them, and re-layouts: 3.77 us -> 1.56 us
  Pallas kernels: 36.6 us -> 35.3 us
    unnamed x4 -> x0, local copies, waits for them, and re-layouts: 2.97 us -> none
    pallas_call x1, Pallas kernels: 36.6 us -> 35.3 us  [shards(): pl.pallas_call(functools.partial(kernel, tx_n, ty_n, pg_n, weight), out_s...]
    pallas_call x1, local copies, waits for them, and re-layouts: 0.1 us -> 0.85 us  [shards(): pl.pallas_call(functools.partial(kernel, tx_n, ty_n, pg_n, weight), out_s...]
where the time goes in v3:
time: 37.1 us; the launch traced here: 36.9 us
  Pallas kernels  35.3 us (95%)
  local copies, waits for them, and re-layouts  1.56 us (4%)
    pallas_call x1, Pallas kernels, shards(): pl.pallas_call(functools.partial(kernel, tx_n, ty_n, pg_n, weight), out_s...  35.3 us
    pallas_call x1, local copies, waits for them, and re-layouts, shards(): pl.pallas_call(functools.partial(kernel, tx_n, ty_n, pg_n, weight), out_s...  0.85 us

profile of v3, /device:TPU:0, one launch (start us, length us, event | category | flops | bytes accessed | tf_op | source)
XLA Modules:
  0.0 36.9 jit_solution(15657896795548218320)
XLA Ops:
  0.0 35.3 %shard_map.37 = f32[32,256]{1,0:T(8,128)} custom-call(s32[8]{0:T(128)} %order_ref.1, bf16[16,3,16,128]{3,2,1,0:T(8,128)(2,1)} %own_any.1, bf16[64,3,16,128]{3,2,1,0:T(8,128)(2,1)} %adj_in.1), custom_call_target="tpu_custom_call" | custom-call | tf_op jit(solution)/shard_map/pallas_call | solution.py:301
  35.4 0.9 %copy.5 = f32[32,256]{0,1:T(8,128)S(1)} copy(f32[32,256]{1,0:T(8,128)} %shard_map.37) | data formatting | bytes 65536 | tf_op jit(solution)/shard_map/pallas_call | solution.py:301
  36.2 0.7 %copy.6 = f32[16,16,32]{2,1,0:T(8,128)} copy(f32[16,16,32]{2,0,1:T(8,128)S(1)} %bitcast.3) | data formatting | bytes 65536 | tf_op jit(solution)/shard_map/transpose | solution.py:336

commit v4 on v3

--- a/solution.py
+++ b/solution.py
@@ -239,7 +239,7 @@
             def _():
                 arrived((sides[1],))
 
-            lax.fori_loop(q * quarter, (q + 1) * quarter, grads, 0)
+            lax.fori_loop(0, quarter, lambda i, c: grads(q * quarter + i, c), 0, unroll=True)
 
         def two(i, carry):
             x0 = q * quarter + 4 * i

time: 37.1 us -> 36.1 us (0.973)
  Pallas kernels: 35.3 us -> 34.3 us
    pallas_call x1, Pallas kernels: 35.3 us -> 34.3 us  [shards(): pl.pallas_call(functools.partial(kernel, tx_n, ty_n, pg_n, weight), out_s...]
where the time goes in v4:
time: 36.1 us; the launch traced here: 35.9 us
  Pallas kernels  34.3 us (95%)
  local copies, waits for them, and re-layouts  1.56 us (4%)
    pallas_call x1, Pallas kernels, shards(): pl.pallas_call(functools.partial(kernel, tx_n, ty_n, pg_n, weight), out_s...  34.3 us
    pallas_call x1, local copies, waits for them, and re-layouts, shards(): pl.pallas_call(functools.partial(kernel, tx_n, ty_n, pg_n, weight), out_s...  0.85 us

profile of v4, /device:TPU:0, one launch (start us, length us, event | category | flops | bytes accessed | tf_op | source)
XLA Modules:
  0.0 35.9 jit_solution(2735320294129750066)
XLA Ops:
  0.0 34.3 %shard_map.37 = f32[32,256]{1,0:T(8,128)} custom-call(s32[8]{0:T(128)} %order_ref.1, bf16[16,3,16,128]{3,2,1,0:T(8,128)(2,1)} %own_any.1, bf16[64,3,16,128]{3,2,1,0:T(8,128)(2,1)} %adj_in.1), custom_call_target="tpu_custom_call" | custom-call | tf_op jit(solution)/shard_map/pallas_call | solution.py:301
  34.3 0.9 %copy.5 = f32[32,256]{0,1:T(8,128)S(1)} copy(f32[32,256]{1,0:T(8,128)} %shard_map.37) | data formatting | bytes 65536 | tf_op jit(solution)/shard_map/pallas_call | solution.py:301
  35.2 0.7 %copy.6 = f32[16,16,32]{2,1,0:T(8,128)} copy(f32[16,16,32]{2,0,1:T(8,128)S(1)} %bitcast.3) | data formatting | bytes 65536 | tf_op jit(solution)/shard_map/transpose | solution.py:336
